TPU v7x, 512 devices: a whole 4x4x16 slice. The times are simulated.
512 devices in a mesh: row: 16 (over x_lo, y, core), col: 32 (over x_hi, z).
Axes of the slice: x: 4 (x_hi: 2, x_lo: 2; x = x_hi * 2 + x_lo), y: 4, z: 16, core: 2. Of those that a mesh axis runs over, the one named last changes fastest.
Arguments:
- inverse_slab: bfloat16 [65536, 8192], P('row', 'col'), may hold values from -0.0234375 to 0.0234375
- cot_solved: bfloat16 [64, 65536], P(None, ('row', 'col')), may hold values from -6 to 6
- cot_direct: bfloat16 [64, 8192], P(None, 'col'), may hold values from -6 to 6
- solved_panel: bfloat16 [64, 65536], P(None, 'col'), may hold values from -1.078125 to 1.078125
Outputs:
- grad_factor: float32 [64, 8192], P(None, 'col')
- grad_operator: bfloat16 [8192, 65536], P('row', 'col')
All inputs are finite; a program needn't handle non-finite values.
Results may differ from a plain program's by a relative error of at most 0.0049.
Values may be sent and summed in bfloat16 or wider, within the bound.
No kernel may reach another device: no remote copies, remote signals or barrier semaphores. Data moves between devices by JAX's collectives and lax.ppermute only.
A program may use at most 64 MiB of HBM per device.

v0:
```python
import jax
import jax.numpy as jnp
from jax import lax
from jax.sharding import PartitionSpec as P


def body(inverse_slab, cot_solved, cot_direct, solved_panel):
    scale = 1.0 / jnp.sqrt(jnp.float32(2.0))
    block_rows = lax.all_gather(cot_solved, "col", axis=1, tiled=True)
    partial_sum = jnp.dot(block_rows, inverse_slab, preferred_element_type=jnp.float32)
    pulled = lax.psum(partial_sum, "row")
    grad_factor = (cot_direct.astype(jnp.float32) + pulled) * scale
    pulled_low = pulled.astype(jnp.bfloat16)
    width = pulled_low.shape[1]
    factor = lax.axis_size("col") // lax.axis_size("row")
    gathered = lax.all_gather(pulled_low, "col", axis=1, tiled=True)
    offset = lax.axis_index("row") * (factor * width)
    needed = lax.dynamic_slice_in_dim(gathered, offset, factor * width, 1)
    product = lax.dot_general(
        needed, solved_panel, (((0,), (0,)), ((), ())), preferred_element_type=jnp.float32
    )
    grad_operator = (product * -scale).astype(jnp.bfloat16)
    return (grad_factor, grad_operator)


def solution(mesh):
    in_specs = (P("row", "col"), P(None, ("row", "col")), P(None, "col"), P(None, "col"))
    out_specs = (P(None, "col"), P("row", "col"))
    return jax.shard_map(body, mesh=mesh, in_specs=in_specs, out_specs=out_specs, check_vma=False)
```

profile of v0, /device:TPU:8, one launch (start us, length us, event | category | flops | bytes accessed | tf_op | source)
XLA Modules:
  0.0 356.7 jit_solution(521984565598067549)
XLA Ops:
  7.2 0.0 copy-start
  7.2 0.0 copy-start.2
  7.2 0.0 copy-start.1
  7.2 0.0 all-reduce.2.cloned.1.call-start
  7.2 85.5 %all_gather.6 = bf16[64,4096]{1,0:T(8,128)(2,1)S(1)} all-gather(bf16[64,128]{1,0:T(8,128)(2,1)} %param.5), channel_id=1, replica_groups=mesh['row'=16,'col'=32] {'col'}, dimensions={1}, use_global_device_ids=true | all-gather | bytes 540672 | tf_op jit(solution)/shard_map/all_gather | solution.py:9
  92.8 0.0 copy-done
  92.8 1.1 fusion.3
  93.8 0.0 all-reduce.2.cloned.1.call-update
  93.9 0.0 all-gather.2.cloned.1.call-start
  93.9 111.6 %all-reduce.2.cloned.1.call-done = f32[64,256]{1,0:T(8,128)} async-done(((f32[64,256]{1,0:T(8,128)}), f32[64,256]{1,0:T(8,128)}) %all-reduce.2.cloned.1.call-update) | async-done | bytes 65552 | tf_op jit(solution)/shard_map/psum | solution.py:11
  205.6 0.0 copy-done.2
  205.6 1.6 fusion.2
  207.1 0.0 all-gather.2.cloned.1.call-update
  207.1 139.8 %all-gather.2.cloned.1.call-done = bf16[64,8192]{1,0:T(8,128)(2,1)} async-done(((bf16[64,256]{1,0:T(8,128)(2,1)}), bf16[64,8192]{1,0:T(8,128)(2,1)}) %all-gather.2.cloned.1.call-update) | async-done | bytes 1048592 | tf_op jit(solution)/shard_map/all_gather | solution.py:16
  347.0 0.0 copy-done.1
  347.0 2.9 multiply_convert_fusion
Async XLA Ops:
  7.2 85.6 %copy-start = (bf16[4096,256]{1,0:T(8,128)(2,1)S(1)}, bf16[4096,256]{1,0:T(8,128)(2,1)}, u32[]{:S(2)}) copy-start(bf16[4096,256]{1,0:T(8,128)(2,1)} %param.4) | copy-start | bytes 6291460
  7.2 198.4 %copy-start.2 = (bf16[64,256]{1,0:T(8,128)(2,1)S(1)}, bf16[64,256]{1,0:T(8,128)(2,1)}, u32[]{:S(2)}) copy-start(bf16[64,256]{1,0:T(8,128)(2,1)} %param.6) | copy-start | bytes 98308
  7.2 339.8 %copy-start.1 = (bf16[64,2048]{1,0:T(8,128)(2,1)S(1)}, bf16[64,2048]{1,0:T(8,128)(2,1)}, u32[]{:S(2)}) copy-start(bf16[64,2048]{1,0:T(8,128)(2,1)} %param.7) | copy-start | bytes 786436
  7.2 198.4 %all-reduce.2.cloned.1.call-start = ((), (), s32[]{:S(2)}) async-start(), calls=%async_computation | async-start | bytes 131072 | tf_op jit(solution)/shard_map/psum | solution.py:11
  93.9 253.1 %all-gather.2.cloned.1.call-start = ((), (), s32[]{:S(2)}) async-start(), calls=%async_computation.1 | async-start | bytes 1081344 | tf_op jit(solution)/shard_map/all_gather | solution.py:16
Sparse Core Ops, SparseCore 0:
  94.0 111.5 all-reduce.1
  209.0 137.8 all-gather.1
where the time goes:
time: 357 us
  waiting for transfers between devices  251 us (70%)
  blocking collectives  85.5 us (24%)
  between operations  14.1 us (4%)
  matrix products  3.98 us (1%)
    all_gather x1, waiting for transfers between devices, body(): gathered = lax.all_gather(pulled_low, 'col', axis=1, tiled=True)  140 us
    psum x1, waiting for transfers between devices, body(): pulled = lax.psum(partial_sum, 'row')  112 us
    all_gather x1, blocking collectives, body(): block_rows = lax.all_gather(cot_solved, 'col', axis=1, tiled=True)  85.5 us
  transfers between devices with their start and end apart: 2, of which 2 were waited for; matrix products, arithmetic and copies ran while one was open for 0% of the time, Pallas kernels for 0%

commit v1 on v0

--- a/solution.py
+++ b/solution.py
@@ -8,7 +8,7 @@
     scale = 1.0 / jnp.sqrt(jnp.float32(2.0))
     block_rows = lax.all_gather(cot_solved, "col", axis=1, tiled=True)
     partial_sum = jnp.dot(block_rows, inverse_slab, preferred_element_type=jnp.float32)
-    pulled = lax.psum(partial_sum, "row")
+    pulled = jnp.sum(lax.all_gather(partial_sum, "row"), axis=0)
     grad_factor = (cot_direct.astype(jnp.float32) + pulled) * scale
     pulled_low = pulled.astype(jnp.bfloat16)
     width = pulled_low.shape[1]

time: 357 us -> 272 us (0.76)
  waiting for transfers between devices: 251 us -> 167 us
    psum x1 -> x0, waiting for transfers between devices: 112 us -> none  [body(): pulled = lax.psum(partial_sum, 'row')]
    all_gather x0 -> x1, waiting for transfers between devices: none -> 28.8 us  [body(): pulled = jnp.sum(lax.all_gather(partial_sum, 'row'), axis=0)]
where the time goes in v1:
time: 272 us
  waiting for transfers between devices  167 us (61%)
  blocking collectives  85.5 us (31%)
  between operations  14.1 us (5%)
  matrix products  3.97 us (1%)
    all_gather x1, waiting for transfers between devices, body(): gathered = lax.all_gather(pulled_low, 'col', axis=1, tiled=True)  138 us
    all_gather x1, blocking collectives, body(): block_rows = lax.all_gather(cot_solved, 'col', axis=1, tiled=True)  85.5 us
    all_gather x1, waiting for transfers between devices, body(): pulled = jnp.sum(lax.all_gather(partial_sum, 'row'), axis=0)  28.8 us
  transfers between devices with their start and end apart: 2, of which 2 were waited for; matrix products, arithmetic and copies ran while one was open for 0% of the time, Pallas kernels for 0%

profile of v1, /device:TPU:8, one launch (start us, length us, event | category | flops | bytes accessed | tf_op | source)
XLA Modules:
  0.0 272.2 jit_solution(1675115861001552905)
XLA Ops:
  7.2 0.0 copy-start
  7.2 0.0 copy-start.2
  7.2 0.0 all-gather.6.cloned.1.call-start
  7.2 85.5 %all_gather.12 = bf16[64,4096]{1,0:T(8,128)(2,1)S(1)} all-gather(bf16[64,128]{1,0:T(8,128)(2,1)} %param.5), channel_id=1, replica_groups=mesh['row'=16,'col'=32] {'col'}, dimensions={1}, use_global_device_ids=true | all-gather | bytes 540672 | tf_op jit(solution)/shard_map/all_gather | solution.py:9
  92.7 0.0 copy-done
  92.7 0.0 copy-start.1
  92.7 1.1 fusion.3
  93.8 0.0 all-gather.6.cloned.1.call-update
  93.9 0.0 all-gather.4.cloned.1.call-start
  93.9 28.8 %all-gather.6.cloned.1.call-done = f32[1024,256]{1,0:T(8,128)} async-done(((f32[64,256]{1,0:T(8,128)}), f32[1024,256]{1,0:T(8,128)}) %all-gather.6.cloned.1.call-update) | async-done | bytes 1048592 | tf_op jit(solution)/shard_map/all_gather | solution.py:11
  122.8 1.3 reduce_sum.9
  124.0 0.0 copy-done.2
  124.1 0.7 fusion.2
  124.7 0.0 all-gather.4.cloned.1.call-update
  124.7 137.7 %all-gather.4.cloned.1.call-done = bf16[64,8192]{1,0:T(8,128)(2,1)} async-done(((bf16[64,256]{1,0:T(8,128)(2,1)}), bf16[64,8192]{1,0:T(8,128)(2,1)}) %all-gather.4.cloned.1.call-update) | async-done | bytes 1048592 | tf_op jit(solution)/shard_map/all_gather | solution.py:16
  262.5 0.0 copy-done.1
  262.5 2.9 %multiply_convert_fusion = bf16[512,2048]{1,0:T(8,128)(2,1)} fusion(bf16[64,2048]{1,0:T(8,128)(2,1)S(1)} %copy-done.1, bf16[64,8192]{1,0:T(8,128)(2,1)} %all-gather.4.cloned.1.call-done, s32[]{:T(128)S(6)} %select_n.3), kind=kOutput, calls=%fused_computation | convolution fusion | flops 136314880 | bytes 2424836 | tf_op jit(solution)/shard_map/dot_general | solution.py:19
Async XLA Ops:
  7.2 85.6 %copy-start = (bf16[4096,256]{1,0:T(8,128)(2,1)S(1)}, bf16[4096,256]{1,0:T(8,128)(2,1)}, u32[]{:S(2)}) copy-start(bf16[4096,256]{1,0:T(8,128)(2,1)} %param.4) | copy-start | bytes 6291460
  7.2 116.9 %copy-start.2 = (bf16[64,256]{1,0:T(8,128)(2,1)S(1)}, bf16[64,256]{1,0:T(8,128)(2,1)}, u32[]{:S(2)}) copy-start(bf16[64,256]{1,0:T(8,128)(2,1)} %param.6) | copy-start | bytes 98308
  7.2 115.6 %all-gather.6.cloned.1.call-start = ((), (), s32[]{:S(2)}) async-start(), calls=%async_computation.1 | async-start | bytes 1114112 | tf_op jit(solution)/shard_map/all_gather | solution.py:11
  92.7 169.7 %copy-start.1 = (bf16[64,2048]{1,0:T(8,128)(2,1)S(1)}, bf16[64,2048]{1,0:T(8,128)(2,1)}, u32[]{:S(2)}) copy-start(bf16[64,2048]{1,0:T(8,128)(2,1)} %param.7) | copy-start | bytes 786436
  93.9 168.6 %all-gather.4.cloned.1.call-start = ((), (), s32[]{:S(2)}) async-start(), calls=%async_computation | async-start | bytes 1081344 | tf_op jit(solution)/shard_map/all_gather | solution.py:16
Sparse Core Ops, SparseCore 0:
  94.0 28.7 all-gather.5
  126.2 136.1 all-gather.3

commit v2 on v0

--- a/solution.py
+++ b/solution.py
@@ -6,7 +6,9 @@
 
 def body(inverse_slab, cot_solved, cot_direct, solved_panel):
     scale = 1.0 / jnp.sqrt(jnp.float32(2.0))
-    block_rows = lax.all_gather(cot_solved, "col", axis=1, tiled=True)
+    block_rows = jnp.concatenate(
+        lax.all_to_all(jnp.stack([cot_solved] * lax.axis_size("col")), "col", 0, 0), axis=1
+    )
     partial_sum = jnp.dot(block_rows, inverse_slab, preferred_element_type=jnp.float32)
     pulled = lax.psum(partial_sum, "row")
     grad_factor = (cot_direct.astype(jnp.float32) + pulled) * scale

time: 357 us -> 325 us (0.910)
  blocking collectives: 85.5 us -> 50.5 us
    all_gather x1 -> x0, blocking collectives: 85.5 us -> none  [body(): block_rows = lax.all_gather(cot_solved, 'col', axis=1, tiled=True)]
    all_to_all x0 -> x1, blocking collectives: none -> 50.5 us  [body(): lax.all_to_all(jnp.stack([cot_solved] * lax.axis_size('col')), 'col', 0, 0)]
where the time goes in v2:
time: 325 us
  waiting for transfers between devices  254 us (78%)
  blocking collectives  50.5 us (16%)
  between operations  14.1 us (4%)
  matrix products  4 us (1%)
    all_gather x1, waiting for transfers between devices, body(): gathered = lax.all_gather(pulled_low, 'col', axis=1, tiled=True)  140 us
    psum x1, waiting for transfers between devices, body(): pulled = lax.psum(partial_sum, 'row')  114 us
    all_to_all x1, blocking collectives, body(): lax.all_to_all(jnp.stack([cot_solved] * lax.axis_size('col')), 'col', 0, 0)  50.5 us
  transfers between devices with their start and end apart: 2, of which 2 were waited for; matrix products, arithmetic and copies ran while one was open for 0% of the time, Pallas kernels for 0%

profile of v2, /device:TPU:8, one launch (start us, length us, event | category | flops | bytes accessed | tf_op | source)
XLA Modules:
  0.0 325.2 jit_solution(10761793197826677998)
XLA Ops:
  7.2 0.0 copy-start
  7.2 0.0 copy-start.2
  7.2 0.0 all-reduce.2.cloned.1.call-start
  7.2 1.0 stack.2
  8.2 0.0 copy-start.1
  8.2 50.5 %all_to_all.5 = bf16[32,64,128]{2,1,0:T(8,128)(2,1)S(1)} all-to-all(bf16[32,64,128]{2,1,0:T(8,128)(2,1)S(1)} %stack.2), channel_id=1, replica_groups=mesh['row'=16,'col'=32] {'col'}, dimensions={0} | all-to-all | bytes 1048576 | tf_op jit(solution)/shard_map/all_to_all | solution.py:10
  58.8 0.0 copy-done
  58.8 1.1 fusion
  59.9 0.0 all-reduce.2.cloned.1.call-update
  59.9 0.0 all-gather.2.cloned.1.call-start
  59.9 114.2 %all-reduce.2.cloned.1.call-done = f32[64,256]{1,0:T(8,128)} async-done(((f32[64,256]{1,0:T(8,128)}), f32[64,256]{1,0:T(8,128)}) %all-reduce.2.cloned.1.call-update) | async-done | bytes 65552 | tf_op jit(solution)/shard_map/psum | solution.py:13
  174.1 0.0 copy-done.2
  174.1 1.6 fusion.5
  175.7 0.0 all-gather.2.cloned.1.call-update
  175.7 139.8 %all-gather.2.cloned.1.call-done = bf16[64,8192]{1,0:T(8,128)(2,1)} async-done(((bf16[64,256]{1,0:T(8,128)(2,1)}), bf16[64,8192]{1,0:T(8,128)(2,1)}) %all-gather.2.cloned.1.call-update) | async-done | bytes 1048592 | tf_op jit(solution)/shard_map/all_gather | solution.py:18
  315.5 0.0 copy-done.1
  315.5 2.9 multiply_convert_fusion
Async XLA Ops:
  7.2 51.6 %copy-start = (bf16[4096,256]{1,0:T(8,128)(2,1)S(1)}, bf16[4096,256]{1,0:T(8,128)(2,1)}, u32[]{:S(2)}) copy-start(bf16[4096,256]{1,0:T(8,128)(2,1)} %param.4) | copy-start | bytes 6291460
  7.2 166.9 %copy-start.2 = (bf16[64,256]{1,0:T(8,128)(2,1)S(1)}, bf16[64,256]{1,0:T(8,128)(2,1)}, u32[]{:S(2)}) copy-start(bf16[64,256]{1,0:T(8,128)(2,1)} %param.6) | copy-start | bytes 98308
  7.2 166.9 %all-reduce.2.cloned.1.call-start = ((), (), s32[]{:S(2)}) async-start(), calls=%async_computation.1 | async-start | bytes 131072 | tf_op jit(solution)/shard_map/psum | solution.py:13
  8.2 307.3 %copy-start.1 = (bf16[64,2048]{1,0:T(8,128)(2,1)S(1)}, bf16[64,2048]{1,0:T(8,128)(2,1)}, u32[]{:S(2)}) copy-start(bf16[64,2048]{1,0:T(8,128)(2,1)} %param.7) | copy-start | bytes 786436
  59.9 255.6 %all-gather.2.cloned.1.call-start = ((), (), s32[]{:S(2)}) async-start(), calls=%async_computation.2 | async-start | bytes 1081344 | tf_op jit(solution)/shard_map/all_gather | solution.py:18
Sparse Core Ops, SparseCore 0:
  60.0 114.0 all-reduce.1
  177.6 137.8 all-gather.1
